TPU v7x, 32 devices: a whole 2x2x4 slice. The times are simulated.
32 devices in a mesh: dp: 8 (over z, x), tensor: 4 (over y, core).
Axes of the slice: x: 2, y: 2, z: 4, core: 2. Of those that a mesh axis runs over, the one named last changes fastest.
Arguments:
- images: bfloat16 [16, 197, 768], P('dp'), may hold values from -6 to 6
- image_counts: int32 [8], P('dp'), may hold values from 1 to 2, as said below
- first_norm_gain: float32 [768], replicated, may hold values from 0.5 to 1.5
- first_norm_bias: float32 [768], replicated, may hold values from -3 to 3
- qkv_weight: bfloat16 [768, 3, 768], P(None, None, 'tensor'), may hold values from -2 to 2
- qv_bias: float32 [2, 768], P(None, 'tensor'), may hold values from -3 to 3
- out_weight: bfloat16 [768, 768], P('tensor'), may hold values from -1.25 to 1.25
- out_bias: float32 [768], replicated, may hold values from -3 to 3
- second_norm_gain: float32 [768], replicated, may hold values from 0.5 to 1.5
- second_norm_bias: float32 [768], replicated, may hold values from -3 to 3
- fc1_weight: bfloat16 [768, 3072], P(None, 'tensor'), may hold values from -0.21875 to 0.21875
- fc1_bias: float32 [3072], P('tensor'), may hold values from -3 to 3
- fc2_weight: bfloat16 [3072, 768], P('tensor'), may hold values from -0.15625 to 0.15625
- fc2_bias: float32 [768], replicated, may hold values from -3 to 3
- cotangent: bfloat16 [16, 197, 768], P('dp'), may hold values from -6 to 6
Outputs:
- block_out: bfloat16 [16, 197, 768], P('dp')
- input_grad: bfloat16 [16, 197, 768], P('dp')
- grad_first_norm_gain: float32 [768], replicated
- grad_first_norm_bias: float32 [768], replicated
- grad_qkv_weight: float32 [768, 3, 768], P(None, None, 'tensor')
- grad_qv_bias: float32 [2, 768], P(None, 'tensor')
- grad_out_weight: float32 [768, 768], P('tensor')
- grad_out_bias: float32 [768], replicated
- grad_second_norm_gain: float32 [768], replicated
- grad_second_norm_bias: float32 [768], replicated
- grad_fc1_weight: float32 [768, 3072], P(None, 'tensor')
- grad_fc1_bias: float32 [3072], P('tensor')
- grad_fc2_weight: float32 [3072, 768], P('tensor')
- grad_fc2_bias: float32 [768], replicated
Inputs may be any that keep to these rules, and one draw needn't show every extreme that they name: `image_counts`: some index of dp has 2 live slots and some has 1; live slots come first in each index's block of 2.
All inputs are finite; a program needn't handle non-finite values.
Results may differ from a plain program's by a relative error of at most 0.02.
Values may be sent and summed in bfloat16 or wider, within the bound.
A program may use at most 128 MiB of HBM per device.

v0:
```python
import jax
import jax.numpy as jnp
from jax import lax
from jax.sharding import PartitionSpec as P

HEAD_DIM = 64
EPS = 1e-06
ROOT_HALF = 0.7071067811865476
INV_ROOT_TAU = 0.3989422804014327


def to_half(array_in):
    return array_in.astype(jnp.bfloat16)


def norm_forward(row_values, gain_vec, shift_vec):
    centre = row_values - jnp.mean(row_values, axis=-1, keepdims=True)
    inverse = lax.rsqrt(jnp.mean(centre * centre, axis=-1, keepdims=True) + EPS)
    scaled = centre * inverse
    return (scaled * gain_vec + shift_vec, scaled, inverse)


def norm_backward(grad_out, scaled, inverse, gain_vec):
    grad_scaled = grad_out * gain_vec
    grad_rows = inverse * (
        grad_scaled
        - jnp.mean(grad_scaled, axis=-1, keepdims=True)
        - scaled * jnp.mean(grad_scaled * scaled, axis=-1, keepdims=True)
    )
    return (grad_rows, jnp.sum(grad_out * scaled, axis=0), jnp.sum(grad_out, axis=0))


def gelu_value(pre_act):
    return 0.5 * pre_act * (1.0 + jax.scipy.special.erf(pre_act * ROOT_HALF))


def gelu_slope(pre_act):
    return (
        0.5 * (1.0 + jax.scipy.special.erf(pre_act * ROOT_HALF))
        + pre_act * jnp.exp(-0.5 * pre_act * pre_act) * INV_ROOT_TAU
    )


def per_device(
    images,
    image_counts,
    first_norm_gain,
    first_norm_bias,
    qkv_weight,
    qv_bias,
    out_weight,
    out_bias,
    second_norm_gain,
    second_norm_bias,
    fc1_weight,
    fc1_bias,
    fc2_weight,
    fc2_bias,
    cotangent,
):
    f32 = jnp.float32
    slot_count, length, model_width = images.shape
    local_width = qkv_weight.shape[2]
    local_heads = local_width // HEAD_DIM
    row_count = slot_count * length
    score_scale = HEAD_DIM ** (-0.5)
    live_slots = (jnp.arange(slot_count, dtype=jnp.int32) < image_counts[0]).astype(f32)
    row_live = jnp.broadcast_to(live_slots[:, None], (slot_count, length)).reshape(row_count, 1)
    head_shape = (slot_count, length, local_heads, HEAD_DIM)
    row_values = images.reshape(row_count, model_width).astype(f32)
    norm_one, scaled_one, inverse_one = norm_forward(row_values, first_norm_gain, first_norm_bias)
    norm_one = to_half(norm_one)
    qkv_flat = qkv_weight.reshape(model_width, 3 * local_width)
    qkv_shift = jnp.stack([qv_bias[0], jnp.zeros_like(qv_bias[0]), qv_bias[1]])
    qkv_rows = to_half(
        jnp.dot(norm_one, qkv_flat, preferred_element_type=f32).reshape(row_count, 3, local_width)
        + qkv_shift
    )
    queries = qkv_rows[:, 0].reshape(head_shape)
    key_heads = qkv_rows[:, 1].reshape(head_shape)
    value_heads = qkv_rows[:, 2].reshape(head_shape)
    scores = (
        jnp.einsum("bqhd,bkhd->bhqk", queries, key_heads, preferred_element_type=f32) * score_scale
    )
    row_peak = jnp.max(scores, axis=-1, keepdims=True)
    log_total = row_peak + jnp.log(jnp.sum(jnp.exp(scores - row_peak), axis=-1, keepdims=True))
    probs_full = jnp.exp(scores - log_total)
    probs_half = to_half(probs_full)
    context = to_half(
        jnp.einsum("bhqk,bkhd->bqhd", probs_half, value_heads, preferred_element_type=f32)
    )
    context_rows = context.reshape(row_count, local_width)
    attn_part = jnp.dot(context_rows, out_weight, preferred_element_type=f32)
    resid_rows = (
        row_values
        + lax.psum(attn_part.astype(jnp.bfloat16), "tensor").astype(jnp.float32)
        + out_bias
    )
    norm_two, scaled_two, inverse_two = norm_forward(resid_rows, second_norm_gain, second_norm_bias)
    norm_two = to_half(norm_two)
    pre_act = jnp.dot(norm_two, fc1_weight, preferred_element_type=f32) + fc1_bias
    act_half = to_half(gelu_value(pre_act))
    mlp_part = jnp.dot(act_half, fc2_weight, preferred_element_type=f32)
    final_rows = (
        resid_rows
        + lax.psum(mlp_part.astype(jnp.bfloat16), "tensor").astype(jnp.float32)
        + fc2_bias
    )
    block_out = to_half(final_rows * row_live).reshape(slot_count, length, model_width)
    inv_images = 1.0 / (slot_count * lax.axis_size("dp"))
    grad_final = cotangent.reshape(row_count, model_width).astype(f32) * row_live
    grad_final_half = to_half(grad_final)
    grad_act = jnp.dot(grad_final_half, fc2_weight.T, preferred_element_type=f32)
    grad_pre = grad_act * gelu_slope(pre_act)
    grad_pre_half = to_half(grad_pre)
    two_part = jnp.dot(grad_pre_half, fc1_weight.T, preferred_element_type=f32)
    grad_norm_two = lax.psum(two_part.astype(jnp.bfloat16), "tensor").astype(jnp.float32)
    back_two, gain_two, shift_two = norm_backward(
        grad_norm_two, scaled_two, inverse_two, second_norm_gain
    )
    mlp_grads = (
        jnp.dot(norm_two.T, grad_pre_half, preferred_element_type=f32) * inv_images,
        jnp.sum(grad_pre, axis=0, keepdims=True) * inv_images,
        jnp.dot(act_half.T, grad_final_half, preferred_element_type=f32) * inv_images,
        jnp.stack([gain_two, shift_two, jnp.sum(grad_final, axis=0)]) * inv_images,
    )
    grad_resid = grad_final + back_two
    grad_resid_half = to_half(grad_resid)
    grad_context = to_half(
        jnp.dot(grad_resid_half, out_weight.T, preferred_element_type=f32)
    ).reshape(head_shape)
    grad_probs = jnp.einsum(
        "bqhd,bkhd->bhqk", grad_context, value_heads, preferred_element_type=f32
    )
    grad_scores = to_half(
        probs_full
        * (grad_probs - jnp.sum(probs_full * grad_probs, axis=-1, keepdims=True))
        * score_scale
    )
    grad_queries = jnp.einsum(
        "bhqk,bkhd->bqhd", grad_scores, key_heads, preferred_element_type=f32
    ).reshape(row_count, local_width)
    grad_keys = jnp.einsum(
        "bhqk,bqhd->bkhd", grad_scores, queries, preferred_element_type=f32
    ).reshape(row_count, local_width)
    grad_values = jnp.einsum(
        "bhqk,bqhd->bkhd", probs_half, grad_context, preferred_element_type=f32
    ).reshape(row_count, local_width)
    grad_qkv_half = to_half(jnp.stack([grad_queries, grad_keys, grad_values], axis=1)).reshape(
        row_count, 3 * local_width
    )
    one_part = jnp.dot(grad_qkv_half, qkv_flat.T, preferred_element_type=f32)
    grad_norm_one = lax.psum(one_part.astype(jnp.bfloat16), "tensor").astype(jnp.float32)
    back_one, gain_one, shift_one = norm_backward(
        grad_norm_one, scaled_one, inverse_one, first_norm_gain
    )
    input_grad = to_half(grad_resid + back_one).reshape(slot_count, length, model_width)
    attn_grads = (
        jnp.dot(norm_one.T, grad_qkv_half, preferred_element_type=f32) * inv_images,
        jnp.stack([jnp.sum(grad_queries, axis=0), jnp.sum(grad_values, axis=0)]) * inv_images,
        jnp.dot(context_rows.T, grad_resid_half, preferred_element_type=f32) * inv_images,
        jnp.stack([gain_one, shift_one, jnp.sum(grad_resid, axis=0)]) * inv_images,
    )
    shares = (
        lax.psum_scatter(attn_grads[0], "dp", scatter_dimension=1, tiled=True),
        lax.psum_scatter(attn_grads[1], "dp", scatter_dimension=1, tiled=True),
        lax.psum_scatter(attn_grads[2], "dp", scatter_dimension=1, tiled=True),
        lax.psum_scatter(attn_grads[3], "dp", scatter_dimension=1, tiled=True),
        lax.psum_scatter(mlp_grads[0], "dp", scatter_dimension=1, tiled=True),
        lax.psum_scatter(mlp_grads[1], "dp", scatter_dimension=1, tiled=True),
        lax.psum_scatter(mlp_grads[2], "dp", scatter_dimension=1, tiled=True),
        lax.psum_scatter(mlp_grads[3], "dp", scatter_dimension=1, tiled=True),
    )
    gathered = (
        lax.all_gather(shares[0].astype(jnp.bfloat16), "dp", axis=1, tiled=True).astype(
            jnp.float32
        ),
        lax.all_gather(shares[1].astype(jnp.bfloat16), "dp", axis=1, tiled=True).astype(
            jnp.float32
        ),
        lax.all_gather(shares[2].astype(jnp.bfloat16), "dp", axis=1, tiled=True).astype(
            jnp.float32
        ),
        lax.all_gather(shares[3].astype(jnp.bfloat16), "dp", axis=1, tiled=True).astype(
            jnp.float32
        ),
        lax.all_gather(shares[4].astype(jnp.bfloat16), "dp", axis=1, tiled=True).astype(
            jnp.float32
        ),
        lax.all_gather(shares[5].astype(jnp.bfloat16), "dp", axis=1, tiled=True).astype(
            jnp.float32
        ),
        lax.all_gather(shares[6].astype(jnp.bfloat16), "dp", axis=1, tiled=True).astype(
            jnp.float32
        ),
        lax.all_gather(shares[7].astype(jnp.bfloat16), "dp", axis=1, tiled=True).astype(
            jnp.float32
        ),
    )
    attn_full = gathered[:4]
    mlp_full = gathered[4:]
    return (
        block_out,
        input_grad,
        attn_full[3][0],
        attn_full[3][1],
        attn_full[0].reshape(model_width, 3, local_width),
        attn_full[1],
        attn_full[2],
        attn_full[3][2],
        mlp_full[3][0],
        mlp_full[3][1],
        mlp_full[0],
        mlp_full[1][0],
        mlp_full[2],
        mlp_full[3][2],
    )


def solution(mesh):
    placed = (
        P("dp", None, None),
        P("dp"),
        P(),
        P(),
        P(None, None, "tensor"),
        P(None, "tensor"),
        P("tensor", None),
        P(),
        P(),
        P(),
        P(None, "tensor"),
        P("tensor"),
        P("tensor", None),
        P(),
        P("dp", None, None),
    )
    return jax.shard_map(
        per_device,
        mesh=mesh,
        in_specs=placed,
        out_specs=(
            P("dp", None, None),
            P("dp", None, None),
            P(),
            P(),
            P(None, None, "tensor"),
            P(None, "tensor"),
            P("tensor", None),
            P(),
            P(),
            P(),
            P(None, "tensor"),
            P("tensor"),
            P("tensor", None),
            P(),
        ),
        check_vma=False,
    )
```

profile of v0, /device:TPU:0, one launch (start us, length us, event | category | flops | bytes accessed | tf_op | source)
XLA Modules:
  0.0 741.2 jit_solution(13153335465204012786)
XLA Ops:
  7.3 1.7 convert_reduce_fusion.2
  9.0 1.2 multiply_reduce_fusion.2
  10.3 1.2 add_convert_fusion.1
  12.3 1.8 fusion.12
  15.3 1.3 fusion.73
  18.6 1.1 reshape.213
  19.7 2.2 convolution_convert_fusion.2
  22.1 1.2 reshape.219
  23.3 1.1 reshape.220
  25.3 33.3 %all-reduce.7.cloned.1.call-done = bf16[394,768]{1,0:T(8,128)(2,1)} async-done(((bf16[394,768]{1,0:T(8,128)(2,1)}), bf16[394,768]{1,0:T(8,128)(2,1)}) %all-reduce.7.cloned.1.call-update) | async-done | bytes 605200 | tf_op jit(solution)/shard_map/psum | solution.py:96
  58.6 1.7 fusion.67
  61.0 1.7 multiply_convert_fusion.1
  62.7 1.5 fusion.76
  65.0 1.5 convolution_convert_fusion
  66.8 2.9 convolution_convert_fusion.1
  69.7 31.1 %all-reduce.9.cloned.1.call-done = bf16[394,768]{1,0:T(8,128)(2,1)} async-done(((bf16[394,768]{1,0:T(8,128)(2,1)}), bf16[394,768]{1,0:T(8,128)(2,1)}) %all-reduce.9.cloned.1.call-update) | async-done | bytes 605200 | tf_op jit(solution)/shard_map/psum | solution.py:117
  100.8 1.8 fusion.26
  103.2 1.0 copy-done.3
  104.3 1.1 convolution_convert_fusion.5
  105.3 1.1 reshape.215
  106.4 1.4 fusion.50
  107.8 4.5 fusion.69
  112.3 3.8 fusion.34
  116.1 1.7 fusion.70
  118.9 1.6 constant_dynamic-update-slice_fusion.2
  120.5 1.8 copy.151
  122.3 1.1 stack_reshape.13
  124.3 1.1 stack_reshape.14
  126.7 2.9 fusion.10
  130.3 3.4 convolution_multiply_fusion.1
  137.3 3.6 convolution_multiply_fusion
  142.0 26.2 %all-reduce.11.cloned.1.call-done = (bf16[394,768]{1,0:T(8,128)(2,1)}, bf16[394,768]{1,0:T(8,128)(2,1)}) async-done(((bf16[394,768]{1,0:T(8,128)(2,1)}, bf16[394,768]{1,0:T(8,128)(2,1)}), (bf16[394,768]{1,0:T(8,128)(2,1)}, bf16[394,768]{1,0:T(8,128)(2,1)})) %all-reduce.11.cloned.1.call-update) | async-done | bytes 1210384 | tf_op jit(solution)/shard_map/psum | solution.py:106
  168.2 2.1 fusion.27
  171.4 2.4 convolution_multiply_fusion.5
  173.9 2.3 copy.172
  177.2 3.1 convolution_multiply_fusion.2
  180.4 61.4 %reduce-scatter.19.cloned.1.call-done = f32[768,96]{0,1:T(8,128)} async-done(((f32[768,768]{0,1:T(8,128)}), f32[768,96]{0,1:T(8,128)}) %reduce-scatter.19.cloned.1.call-update) | async-done | bytes 294928 | tf_op jit(solution)/shard_map/reduce_scatter | solution.py:169
  241.7 1.6 convert_element_type.193
  245.3 60.9 %reduce-scatter.29.cloned.1.call-done = f32[96,1]{1,0:T(8,128)} async-done(((f32[768,1]{1,0:T(8,128)}), f32[96,1]{1,0:T(8,128)}) %reduce-scatter.29.cloned.1.call-update) | async-done | bytes 400
  307.3 19.5 %all-reduce = bf16[768]{0:T(1024)(128)(2,1)S(1)} all-reduce(bf16[768]{0:T(1024)(128)(2,1)S(1)} %dynamic-update-slice), channel_id=1, replica_groups=mesh['dp'=8,'tensor'=4] {'dp'}, use_global_device_ids=true, to_apply=%add | all-reduce | flops 768 | bytes 3072
  327.6 17.2 %all-reduce.1 = bf16[2,192]{1,0:T(2,128)(2,1)S(1)} all-reduce(f32[2,192]{1,0:T(2,128)S(1)} %maximum_multiply_fusion.2), channel_id=4, replica_groups=mesh['dp'=8,'tensor'=4] {'dp'}, use_global_device_ids=true, to_apply=%region_22.0.clone | all-reduce | flops 384 | bytes 2304
  344.8 18.3 %all-gather.1 = bf16[8,24,2]{1,2,0:T(2,128)(2,1)S(1)} all-gather(bf16[1,24,2]{1,2,0:T(2,128)(2,1)S(1)} %fusion.60), channel_id=1, replica_groups=mesh['dp'=8,'tensor'=4] {'dp'}, dimensions={0}, use_global_device_ids=true | all-gather | bytes 864 | tf_op jit(solution)/shard_map/all_gather | solution.py:178
  363.8 7.4 %reduce-scatter.27.cloned.1.call-done = f32[96,3]{1,0:T(8,128)} async-done(((f32[768,3]{1,0:T(8,128)}), f32[96,3]{1,0:T(8,128)}) %reduce-scatter.27.cloned.1.call-update) | async-done | bytes 1168
  372.1 19.0 %all-gather.2 = bf16[8,96,3]{1,2,0:T(4,128)(2,1)S(1)} all-gather(bf16[1,96,3]{1,2,0:T(4,128)(2,1)S(1)} %bitcast.107), channel_id=1, replica_groups=mesh['dp'=8,'tensor'=4] {'dp'}, dimensions={0}, use_global_device_ids=true | all-gather | bytes 5184 | tf_op jit(solution)/shard_map/all_gather | solution.py:196
  391.1 52.8 %reduce-scatter.21.cloned.1.call-done = f32[768,96]{0,1:T(8,128)} async-done(((f32[768,768]{0,1:T(8,128)}), f32[768,96]{0,1:T(8,128)}) %reduce-scatter.21.cloned.1.call-update) | async-done | bytes 294928 | tf_op jit(solution)/shard_map/reduce_scatter | solution.py:171
  443.9 1.6 convert_element_type.196
  446.3 2.2 multiply_convert_fusion
  448.5 2.1 reshape.214
  450.6 2.5 copy.159
  453.1 1.3 fusion.16
  454.4 1.2 reshape.216
  455.6 1.3 copy.160
  456.9 51.7 %reduce-scatter.23.cloned.1.call-done = f32[96,3]{1,0:T(8,128)} async-done(((f32[768,3]{1,0:T(8,128)}), f32[96,3]{1,0:T(8,128)}) %reduce-scatter.23.cloned.1.call-update) | async-done | bytes 1168
  509.4 18.7 %all-gather = bf16[8,96,3]{1,2,0:T(4,128)(2,1)S(1)} all-gather(bf16[1,96,3]{1,2,0:T(4,128)(2,1)S(1)} %bitcast.108), channel_id=1, replica_groups=mesh['dp'=8,'tensor'=4] {'dp'}, dimensions={0}, use_global_device_ids=true | all-gather | bytes 5184 | tf_op jit(solution)/shard_map/all_gather | solution.py:184
  528.8 45.3 %reduce-scatter.25.cloned.1.call-done = f32[96,192]{1,0:T(8,128)} async-done(((f32[768,192]{1,0:T(8,128)}), f32[96,192]{1,0:T(8,128)}) %reduce-scatter.25.cloned.1.call-update) | async-done | bytes 73744
  574.1 1.0 copy.173
  575.2 31.8 %all_gather.27 = bf16[192,768]{0,1:T(8,128)(2,1)S(1)} all-gather(bf16[192,96]{0,1:T(8,128)(2,1)S(1)} %copy.157), channel_id=1, replica_groups=mesh['dp'=8,'tensor'=4] {'dp'}, dimensions={1}, use_global_device_ids=true | all-gather | bytes 331776 | tf_op jit(solution)/shard_map/all_gather | solution.py:181
  608.0 36.5 %reduce-scatter.17.cloned.1.call-done = f32[768,72]{0,1:T(8,128)} async-done(((f32[768,576]{0,1:T(8,128)}), f32[768,72]{0,1:T(8,128)}) %reduce-scatter.17.cloned.1.call-update) | async-done | bytes 221200 | tf_op jit(solution)/shard_map/reduce_scatter | solution.py:165
  645.4 33.5 %all_gather.25 = bf16[768,576]{0,1:T(8,128)(2,1)S(1)} all-gather(bf16[768,72]{0,1:T(8,128)(2,1)S(1)} %convert_element_type.185), channel_id=1, replica_groups=mesh['dp'=8,'tensor'=4] {'dp'}, dimensions={1}, use_global_device_ids=true | all-gather | bytes 995328 | tf_op jit(solution)/shard_map/all_gather | solution.py:175
  678.9 1.4 convert.20
  680.3 8.9 %all-gather.6.cloned.1.call-done = bf16[768,768]{0,1:T(8,128)(2,1)} async-done(((bf16[768,96]{0,1:T(8,128)(2,1)}), bf16[768,768]{0,1:T(8,128)(2,1)}) %all-gather.6.cloned.1.call-update) | async-done | bytes 1179664 | tf_op jit(solution)/shard_map/all_gather | solution.py:187
  689.1 2.7 copy.162
  691.9 39.8 %all-gather.8.cloned.1.call-done = bf16[768,768]{0,1:T(8,128)(2,1)} async-done(((bf16[768,96]{0,1:T(8,128)(2,1)}), bf16[768,768]{0,1:T(8,128)(2,1)}) %all-gather.8.cloned.1.call-update) | async-done | bytes 1179664 | tf_op jit(solution)/shard_map/all_gather | solution.py:193
  731.6 2.7 copy.163
  (172 shorter events, 25.8 us)
Async XLA Ops:
  7.2 53.4 %copy-start = (bf16[768,768]{1,0:T(8,128)(2,1)S(1)}, bf16[768,768]{1,0:T(8,128)(2,1)}, u32[]{:S(2)}) copy-start(bf16[768,768]{1,0:T(8,128)(2,1)} %param.25) | copy-start | bytes 3538948
  7.2 1.8 copy-start.7
  7.2 3.0 copy-start.24
  7.2 3.0 copy-start.22
  7.2 51.3 %all-reduce.7.cloned.1.call-start = ((), (), s32[]{:S(2)}) async-start(), calls=%async_computation.7 | async-start | bytes 1228800 | tf_op jit(solution)/shard_map/psum | solution.py:96
  10.2 1.3 copy-start.16
  11.5 0.7 copy-start.30
  11.6 2.6 copy-start.8
  14.5 2.4 copy-start.18
  16.7 1.0 copy-start.1
  19.6 2.3 copy-start.13
  21.9 78.9 %all-reduce.9.cloned.1.call-start = ((), (), s32[]{:S(2)}) async-start(), calls=%async_computation.8 | async-start | bytes 1228800 | tf_op jit(solution)/shard_map/psum | solution.py:117
  22.1 1.2 copy-start.12
  23.3 35.3 %copy-start.25 = (f32[768]{0:T(1024)S(1)}, f32[768]{0:T(1024)}, u32[]{:S(2)}) copy-start(f32[768]{0:T(1024)} %param.22) | copy-start | bytes 9220
  25.1 35.1 %copy-start.31 = (f32[2]{0:T(128)}, f32[2]{0:T(128)S(1)}, u32[]{:S(2)}) copy-start(f32[2]{0:T(128)S(1)} %compare_convert_fusion) | copy-start | bytes 28
  60.3 0.7 copy-start.23
  60.3 0.7 copy-start.34
  60.3 0.7 copy-start.35
  61.0 1.7 copy-start.5
  61.0 1.7 copy-start.33
  64.2 0.8 copy-start.37
  66.5 101.7 %all-reduce.11.cloned.1.call-start = ((), (), s32[]{:S(2)}) async-start(), calls=%async_computation.18 | async-start | bytes 2457600 | tf_op jit(solution)/shard_map/psum | solution.py:106
  100.8 1.9 copy-start.6
  100.8 1.9 copy-start.11
  102.7 1.6 copy-start.15
  103.2 1.1 copy-start.3
  107.8 4.5 copy-start.19
  116.1 1.7 copy-start.21
  129.6 0.7 copy-start.36
  129.6 112.1 %reduce-scatter.19.cloned.1.call-start = ((), (), s32[]{:S(2)}) async-start(), calls=%async_computation.10 | async-start | bytes 2654208 | tf_op jit(solution)/shard_map/reduce_scatter | solution.py:169
  133.7 0.7 copy-start.32
  133.7 1.5 copy-start.27
  133.7 172.5 %reduce-scatter.29.cloned.1.call-start = ((), (), s32[]{:S(2)}) async-start(), calls=%async_computation.17 | async-start | bytes 442368
  135.2 2.1 copy-start.20
  136.2 235.0 %reduce-scatter.27.cloned.1.call-start = ((), (), s32[]{:S(2)}) async-start(), calls=%async_computation.16 | async-start | bytes 442368
  137.2 306.7 %reduce-scatter.21.cloned.1.call-start = ((), (), s32[]{:S(2)}) async-start(), calls=%async_computation.12 | async-start | bytes 2654208 | tf_op jit(solution)/shard_map/reduce_scatter | solution.py:171
  140.9 0.9 copy-start.17
  140.9 367.6 %reduce-scatter.23.cloned.1.call-start = ((), (), s32[]{:S(2)}) async-start(), calls=%async_computation.14 | async-start | bytes 442368
  168.2 3.2 copy-start.14
  171.4 402.7 %reduce-scatter.25.cloned.1.call-start = ((), (), s32[]{:S(2)}) async-start(), calls=%async_computation.15 | async-start | bytes 884736
  173.9 2.4 copy-start.9
  176.2 468.3 %reduce-scatter.17.cloned.1.call-start = ((), (), s32[]{:S(2)}) async-start(), calls=%async_computation.9 | async-start | bytes 1990656 | tf_op jit(solution)/shard_map/reduce_scatter | solution.py:165
  180.3 63.2 %copy-start.28 = (u32[32]{0:T(128)S(1)}, u32[32]{0:T(128)}, u32[]{:S(2)}) copy-start(u32[32]{0:T(128)} %constant.41) | copy-start | bytes 388
  180.3 147.2 %copy-start.29 = (f32[3,64]{1,0:T(4,128)S(1)}, f32[3,64]{1,0:T(4,128)}, u32[]{:S(2)}) copy-start(f32[3,64]{1,0:T(4,128)} %get-tuple-element.107) | copy-start | bytes 2308
  180.3 266.0 %copy-start.26 = (f32[768]{0:T(1024)S(1)}, f32[768]{0:T(1024)}, u32[]{:S(2)}) copy-start(f32[768]{0:T(1024)} %param.28) | copy-start | bytes 9220
  180.3 508.8 %all-gather.6.cloned.1.call-start = ((), (), s32[]{:S(2)}) async-start(), calls=%async_computation.11 | async-start | bytes 1327104 | tf_op jit(solution)/shard_map/all_gather | solution.py:187
  243.4 488.2 %all-gather.8.cloned.1.call-start = ((), (), s32[]{:S(2)}) async-start(), calls=%async_computation.13 | async-start | bytes 1327104 | tf_op jit(solution)/shard_map/all_gather | solution.py:193
  446.3 6.7 copy-start.10
  448.5 4.6 copy-start.2
  450.6 2.5 copy-start.4
Sparse Core Ops, SparseCore 0:
  22.0 36.4 all-reduce.6
  66.6 34.0 all-reduce.8
  129.7 38.4 all-reduce.10
  172.1 69.5 reduce-scatter.18
  244.8 61.3 reduce-scatter.28
  309.9 61.2 reduce-scatter.26
  375.3 68.6 reduce-scatter.20
  447.2 61.3 reduce-scatter.22
  511.9 62.2 reduce-scatter.24
  578.0 66.4 reduce-scatter.16
  646.7 42.4 all-gather.5
  691.2 40.3 all-gather.7
where the time goes:
time: 743 us; the launch traced here: 741 us
  waiting for transfers between devices  455 us (61%)
  blocking collectives  158 us (21%)
  local copies, waits for them, and re-layouts  47.1 us (6%)
  matrix products  41.1 us (6%)
  other arithmetic  22.2 us (3%)
  between operations  16.8 us (2%)
    unnamed x16, waiting for transfers between devices  166 us
    reduce_scatter x1, waiting for transfers between devices, per_device(): lax.psum_scatter(mlp_grads[0], 'dp', scatter_dimension=1, tiled=True)  61.4 us
    reduce_scatter x1, waiting for transfers between devices, per_device(): lax.psum_scatter(mlp_grads[2], 'dp', scatter_dimension=1, tiled=True)  52.8 us
    all_gather x1, waiting for transfers between devices, per_device(): lax.all_gather(shares[6].astype(jnp.bfloat16), 'dp', axis=1, tiled=True)  39.8 us
    unnamed x2, blocking collectives  36.6 us
    reduce_scatter x1, waiting for transfers between devices, per_device(): lax.psum_scatter(attn_grads[0], 'dp', scatter_dimension=1, tiled=True)  36.5 us
    all_gather x1, blocking collectives, per_device(): lax.all_gather(shares[0].astype(jnp.bfloat16), 'dp', axis=1, tiled=True)  33.5 us
    psum x1, waiting for transfers between devices, per_device(): lax.psum(attn_part.astype(jnp.bfloat16), 'tensor').astype(jnp.float32)  33.3 us
  transfers between devices with their start and end apart: 12, of which 12 were waited for; matrix products, arithmetic and copies ran while one was open for 7% of the time, Pallas kernels for 0%

commit v1 on v0

--- a/solution.py
+++ b/solution.py
@@ -7,6 +7,18 @@
 EPS = 1e-06
 ROOT_HALF = 0.7071067811865476
 INV_ROOT_TAU = 0.3989422804014327
+
+
+def doubled_up(x, axis, dim):
+    ways, here, hop = (lax.axis_size(axis), lax.axis_index(axis), x.shape[dim])
+    line, have = (x, 1)
+    while have < ways:
+        line = jnp.concatenate(
+            [line, lax.ppermute(line, axis, [(d, (d - have) % ways) for d in range(ways)])],
+            axis=dim,
+        )
+        have = 2 * have
+    return jnp.roll(line, here * hop, axis=dim)
 
 
 def to_half(array_in):
@@ -190,9 +202,7 @@
         lax.all_gather(shares[5].astype(jnp.bfloat16), "dp", axis=1, tiled=True).astype(
             jnp.float32
         ),
-        lax.all_gather(shares[6].astype(jnp.bfloat16), "dp", axis=1, tiled=True).astype(
-            jnp.float32
-        ),
+        doubled_up(shares[6].astype(jnp.bfloat16), "dp", 1).astype(jnp.float32),
         lax.all_gather(shares[7].astype(jnp.bfloat16), "dp", axis=1, tiled=True).astype(
             jnp.float32
         ),

time: 743 us -> 720 us (0.969)
  waiting for transfers between devices: 455 us -> 407 us
  blocking collectives: 158 us -> 180 us
    all_gather x1 -> x0, waiting for transfers between devices: 39.8 us -> none  [per_device(): lax.all_gather(shares[6].astype(jnp.bfloat16), 'dp', axis=1, tiled=True)]
    all_gather x1, blocking collectives: 33.5 us -> 55.4 us  [per_device(): lax.all_gather(shares[0].astype(jnp.bfloat16), 'dp', axis=1, tiled=True)]
    all_gather x1, waiting for transfers between devices: 8.89 us -> 0.01 us  [per_device(): lax.all_gather(shares[4].astype(jnp.bfloat16), 'dp', axis=1, tiled=True)]
    reduce_scatter x1, waiting for transfers between devices: 61.4 us -> 53 us  [per_device(): lax.psum_scatter(mlp_grads[0], 'dp', scatter_dimension=1, tiled=True)]
    unnamed x16 -> x15, waiting for transfers between devices: 166 us -> 173 us
    unnamed x97 -> x105, local copies, waits for them, and re-layouts: 26.6 us -> 27.6 us
  transfers between devices with their start and end apart: 12 -> 14, of which waited for: 12 -> 10; matrix products, arithmetic and copies ran while one was open for 7% -> 7% of each run, Pallas kernels for 0% -> 0%
where the time goes in v1:
time: 720 us; the launch traced here: 719 us
  waiting for transfers between devices  407 us (57%)
  blocking collectives  180 us (25%)
  local copies, waits for them, and re-layouts  45 us (6%)
  matrix products  40.1 us (6%)
  other arithmetic  24.8 us (3%)
  between operations  16.6 us (2%)
    unnamed x15, waiting for transfers between devices  173 us
    all_gather x1, blocking collectives, per_device(): lax.all_gather(shares[0].astype(jnp.bfloat16), 'dp', axis=1, tiled=True)  55.4 us
    reduce_scatter x1, waiting for transfers between devices, per_device(): lax.psum_scatter(mlp_grads[0], 'dp', scatter_dimension=1, tiled=True)  53 us
    reduce_scatter x1, waiting for transfers between devices, per_device(): lax.psum_scatter(mlp_grads[2], 'dp', scatter_dimension=1, tiled=True)  49.1 us
    unnamed x2, blocking collectives  36.6 us
    reduce_scatter x1, waiting for transfers between devices, per_device(): lax.psum_scatter(attn_grads[0], 'dp', scatter_dimension=1, tiled=True)  36.4 us
    psum x1, waiting for transfers between devices, per_device(): lax.psum(attn_part.astype(jnp.bfloat16), 'tensor').astype(jnp.float32)  33.3 us
    all_gather x1, blocking collectives, per_device(): lax.all_gather(shares[2].astype(jnp.bfloat16), 'dp', axis=1, tiled=True)  31.5 us
  transfers between devices with their start and end apart: 14, of which 10 were waited for; matrix products, arithmetic and copies ran while one was open for 7% of the time, Pallas kernels for 0%

profile of v1, /device:TPU:0, one launch (start us, length us, event | category | flops | bytes accessed | tf_op | source)
XLA Modules:
  0.0 718.7 jit_solution(4626761691306035626)
XLA Ops:
  7.3 1.7 convert_reduce_fusion.2
  9.0 1.2 multiply_reduce_fusion.2
  10.3 1.2 add_convert_fusion.1
  12.3 1.8 fusion.12
  15.3 1.3 fusion.73
  18.6 1.1 reshape.213
  19.7 2.2 convolution_convert_fusion.2
  22.1 1.2 reshape.219
  23.3 1.1 reshape.220
  25.3 33.3 %all-reduce.7.cloned.1.call-done = bf16[394,768]{1,0:T(8,128)(2,1)} async-done(((bf16[394,768]{1,0:T(8,128)(2,1)}), bf16[394,768]{1,0:T(8,128)(2,1)}) %all-reduce.7.cloned.1.call-update) | async-done | bytes 605200 | tf_op jit(solution)/shard_map/psum | solution.py:108
  58.6 1.7 fusion.67
  61.0 1.7 multiply_convert_fusion.1
  62.7 1.5 fusion.76
  65.0 1.5 convolution_convert_fusion
  66.8 2.9 convolution_convert_fusion.1
  69.7 31.1 %all-reduce.9.cloned.1.call-done = bf16[394,768]{1,0:T(8,128)(2,1)} async-done(((bf16[394,768]{1,0:T(8,128)(2,1)}), bf16[394,768]{1,0:T(8,128)(2,1)}) %all-reduce.9.cloned.1.call-update) | async-done | bytes 605200 | tf_op jit(solution)/shard_map/psum | solution.py:129
  100.8 1.8 fusion.26
  103.2 1.0 copy-done.2
  104.3 1.1 convolution_convert_fusion.5
  105.3 1.1 reshape.215
  106.4 1.4 fusion.50
  107.8 4.5 fusion.69
  112.3 3.8 fusion.34
  116.1 1.7 fusion.70
  118.9 1.6 constant_dynamic-update-slice_fusion.2
  120.5 1.8 copy.151
  122.3 1.1 stack_reshape.13
  124.3 1.1 stack_reshape.14
  126.7 2.9 fusion.10
  133.2 3.6 convolution_multiply_fusion
  137.9 30.3 %all-reduce.11.cloned.1.call-done = (bf16[394,768]{1,0:T(8,128)(2,1)}, bf16[394,768]{1,0:T(8,128)(2,1)}) async-done(((bf16[394,768]{1,0:T(8,128)(2,1)}, bf16[394,768]{1,0:T(8,128)(2,1)}), (bf16[394,768]{1,0:T(8,128)(2,1)}, bf16[394,768]{1,0:T(8,128)(2,1)})) %all-reduce.11.cloned.1.call-update) | async-done | bytes 1210384 | tf_op jit(solution)/shard_map/psum | solution.py:118
  168.3 2.2 fusion.27
  171.5 2.4 convolution_multiply_fusion.1
  174.8 2.4 convolution_multiply_fusion.5
  177.2 2.3 copy.172
  180.6 3.1 convolution_multiply_fusion.2
  186.2 47.5 %reduce-scatter.29.cloned.1.call-done = f32[96,1]{1,0:T(8,128)} async-done(((f32[768,1]{1,0:T(8,128)}), f32[96,1]{1,0:T(8,128)}) %reduce-scatter.29.cloned.1.call-update) | async-done | bytes 400
  234.8 19.5 %all-reduce = bf16[768]{0:T(1024)(128)(2,1)S(1)} all-reduce(bf16[768]{0:T(1024)(128)(2,1)S(1)} %dynamic-update-slice), channel_id=1, replica_groups=mesh['dp'=8,'tensor'=4] {'dp'}, use_global_device_ids=true, to_apply=%add | all-reduce | flops 768 | bytes 3072
  255.0 17.1 %all-reduce.1 = bf16[2,192]{1,0:T(2,128)(2,1)S(1)} all-reduce(f32[2,192]{1,0:T(2,128)S(1)} %maximum_multiply_fusion.2), channel_id=4, replica_groups=mesh['dp'=8,'tensor'=4] {'dp'}, use_global_device_ids=true, to_apply=%region_22.0.clone | all-reduce | flops 384 | bytes 2304
  272.2 18.3 %all-gather.1 = bf16[8,24,2]{1,2,0:T(2,128)(2,1)S(1)} all-gather(bf16[1,24,2]{1,2,0:T(2,128)(2,1)S(1)} %fusion.60), channel_id=1, replica_groups=mesh['dp'=8,'tensor'=4] {'dp'}, dimensions={0}, use_global_device_ids=true | all-gather | bytes 864 | tf_op jit(solution)/shard_map/all_gather | solution.py:190
  291.2 7.5 %reduce-scatter.27.cloned.1.call-done = f32[96,3]{1,0:T(8,128)} async-done(((f32[768,3]{1,0:T(8,128)}), f32[96,3]{1,0:T(8,128)}) %reduce-scatter.27.cloned.1.call-update) | async-done | bytes 1168
  299.6 19.0 %all-gather.2 = bf16[8,96,3]{1,2,0:T(4,128)(2,1)S(1)} all-gather(bf16[1,96,3]{1,2,0:T(4,128)(2,1)S(1)} %bitcast.107), channel_id=1, replica_groups=mesh['dp'=8,'tensor'=4] {'dp'}, dimensions={0}, use_global_device_ids=true | all-gather | bytes 5184 | tf_op jit(solution)/shard_map/all_gather | solution.py:206
  319.3 3.0 fusion.16
  322.3 49.1 %reduce-scatter.21.cloned.1.call-done = f32[768,96]{0,1:T(8,128)} async-done(((f32[768,768]{0,1:T(8,128)}), f32[768,96]{0,1:T(8,128)}) %reduce-scatter.21.cloned.1.call-update) | async-done | bytes 294928 | tf_op jit(solution)/shard_map/reduce_scatter | solution.py:183
  371.4 1.6 constant_dynamic-update-slice_fusion.10
  373.1 2.1 collective-permute-start
  375.1 1.3 multiply_convert_fusion
  376.6 1.3 copy.159
  378.0 1.3 copy.160
  379.3 56.8 %reduce-scatter.23.cloned.1.call-done = f32[96,3]{1,0:T(8,128)} async-done(((f32[768,3]{1,0:T(8,128)}), f32[96,3]{1,0:T(8,128)}) %reduce-scatter.23.cloned.1.call-update) | async-done | bytes 1168
  436.9 18.8 %all-gather = bf16[8,96,3]{1,2,0:T(4,128)(2,1)S(1)} all-gather(bf16[1,96,3]{1,2,0:T(4,128)(2,1)S(1)} %bitcast.108), channel_id=1, replica_groups=mesh['dp'=8,'tensor'=4] {'dp'}, dimensions={0}, use_global_device_ids=true | all-gather | bytes 5184 | tf_op jit(solution)/shard_map/all_gather | solution.py:196
  455.8 53.0 %reduce-scatter.19.cloned.1.call-done = f32[768,96]{0,1:T(8,128)} async-done(((f32[768,768]{0,1:T(8,128)}), f32[768,96]{0,1:T(8,128)}) %reduce-scatter.19.cloned.1.call-update) | async-done | bytes 294928 | tf_op jit(solution)/shard_map/reduce_scatter | solution.py:181
  508.7 1.6 convert_element_type.193
  510.4 2.0 collective-permute-start.1
  513.2 61.4 %reduce-scatter.25.cloned.1.call-done = f32[96,192]{1,0:T(8,128)} async-done(((f32[768,192]{1,0:T(8,128)}), f32[96,192]{1,0:T(8,128)}) %reduce-scatter.25.cloned.1.call-update) | async-done | bytes 73744
  574.6 1.0 copy.173
  575.7 31.5 %all_gather.24 = bf16[192,768]{0,1:T(8,128)(2,1)S(1)} all-gather(bf16[192,96]{0,1:T(8,128)(2,1)S(1)} %copy.157), channel_id=1, replica_groups=mesh['dp'=8,'tensor'=4] {'dp'}, dimensions={1}, use_global_device_ids=true | all-gather | bytes 331776 | tf_op jit(solution)/shard_map/all_gather | solution.py:193
  608.2 36.4 %reduce-scatter.17.cloned.1.call-done = f32[768,72]{0,1:T(8,128)} async-done(((f32[768,576]{0,1:T(8,128)}), f32[768,72]{0,1:T(8,128)}) %reduce-scatter.17.cloned.1.call-update) | async-done | bytes 221200 | tf_op jit(solution)/shard_map/reduce_scatter | solution.py:177
  645.6 1.2 collective-permute-start.2
  646.8 55.4 %all_gather.22 = bf16[768,576]{0,1:T(8,128)(2,1)S(1)} all-gather(bf16[768,72]{0,1:T(8,128)(2,1)S(1)} %convert_element_type.185), channel_id=1, replica_groups=mesh['dp'=8,'tensor'=4] {'dp'}, dimensions={1}, use_global_device_ids=true | all-gather | bytes 995328 | tf_op jit(solution)/shard_map/all_gather | solution.py:187
  702.2 1.4 convert.20
  704.8 1.6 dynamic-slice_convert_fusion
  706.4 3.0 copy.163
  709.5 2.7 copy.162
  (187 shorter events, 28.0 us)
Async XLA Ops:
  7.2 53.4 %copy-start = (bf16[768,768]{1,0:T(8,128)(2,1)S(1)}, bf16[768,768]{1,0:T(8,128)(2,1)}, u32[]{:S(2)}) copy-start(bf16[768,768]{1,0:T(8,128)(2,1)} %param.25) | copy-start | bytes 3538948
  7.2 1.8 copy-start.5
  7.2 3.0 copy-start.24
  7.2 3.0 copy-start.22
  7.2 51.3 %all-reduce.7.cloned.1.call-start = ((), (), s32[]{:S(2)}) async-start(), calls=%async_computation.7 | async-start | bytes 1228800 | tf_op jit(solution)/shard_map/psum | solution.py:108
  10.2 1.3 copy-start.15
  11.5 0.7 copy-start.30
  11.6 2.6 copy-start.6
  14.5 2.4 copy-start.17
  16.7 1.0 copy-start.1
  19.6 2.3 copy-start.12
  21.9 78.9 %all-reduce.9.cloned.1.call-start = ((), (), s32[]{:S(2)}) async-start(), calls=%async_computation.8 | async-start | bytes 1228800 | tf_op jit(solution)/shard_map/psum | solution.py:129
  22.1 1.2 copy-start.11
  23.3 35.3 %copy-start.25 = (f32[768]{0:T(1024)S(1)}, f32[768]{0:T(1024)}, u32[]{:S(2)}) copy-start(f32[768]{0:T(1024)} %param.22) | copy-start | bytes 9220
  25.1 35.1 %copy-start.31 = (f32[2]{0:T(128)}, f32[2]{0:T(128)S(1)}, u32[]{:S(2)}) copy-start(f32[2]{0:T(128)S(1)} %compare_convert_fusion) | copy-start | bytes 28
  60.3 0.7 copy-start.23
  60.3 0.7 copy-start.34
  60.3 0.7 copy-start.35
  61.0 1.7 copy-start.3
  61.0 1.7 copy-start.33
  64.2 0.8 copy-start.37
  66.5 101.7 %all-reduce.11.cloned.1.call-start = ((), (), s32[]{:S(2)}) async-start(), calls=%async_computation.17 | async-start | bytes 2457600 | tf_op jit(solution)/shard_map/psum | solution.py:118
  100.8 1.9 copy-start.4
  100.8 1.9 copy-start.10
  102.7 1.6 copy-start.14
  103.2 1.1 copy-start.2
  107.8 4.5 copy-start.18
  116.1 1.7 copy-start.21
  129.6 0.7 copy-start.32
  129.6 1.5 copy-start.27
  129.6 104.0 %reduce-scatter.29.cloned.1.call-start = ((), (), s32[]{:S(2)}) async-start(), calls=%async_computation.16 | async-start | bytes 442368
  131.1 2.1 copy-start.20
  132.1 166.6 %reduce-scatter.27.cloned.1.call-start = ((), (), s32[]{:S(2)}) async-start(), calls=%async_computation.15 | async-start | bytes 442368
  133.1 238.3 %reduce-scatter.21.cloned.1.call-start = ((), (), s32[]{:S(2)}) async-start(), calls=%async_computation.12 | async-start | bytes 2654208 | tf_op jit(solution)/shard_map/reduce_scatter | solution.py:183
  136.8 0.9 copy-start.16
  136.8 299.3 %reduce-scatter.23.cloned.1.call-start = ((), (), s32[]{:S(2)}) async-start(), calls=%async_computation.13 | async-start | bytes 442368
  168.2 3.2 copy-start.36
  168.2 3.3 copy-start.38
  171.4 337.3 %reduce-scatter.19.cloned.1.call-start = ((), (), s32[]{:S(2)}) async-start(), calls=%async_computation.10 | async-start | bytes 2654208 | tf_op jit(solution)/shard_map/reduce_scatter | solution.py:181
  173.9 0.9 copy-start.13
  173.9 400.7 %reduce-scatter.25.cloned.1.call-start = ((), (), s32[]{:S(2)}) async-start(), calls=%async_computation.14 | async-start | bytes 884736
  177.2 2.4 copy-start.7
  179.5 465.0 %reduce-scatter.17.cloned.1.call-start = ((), (), s32[]{:S(2)}) async-start(), calls=%async_computation.9 | async-start | bytes 1990656 | tf_op jit(solution)/shard_map/reduce_scatter | solution.py:177
  183.6 0.7 copy-start.28
  183.6 71.3 %copy-start.29 = (f32[3,64]{1,0:T(4,128)S(1)}, f32[3,64]{1,0:T(4,128)}, u32[]{:S(2)}) copy-start(f32[3,64]{1,0:T(4,128)} %get-tuple-element.109) | copy-start | bytes 2308
  183.6 135.6 %copy-start.8 = (bf16[394,768]{1,0:T(8,128)(2,1)S(1)}, bf16[394,768]{1,0:T(8,128)(2,1)}, u32[]{:S(2)}) copy-start(bf16[394,768]{1,0:T(8,128)(2,1)} %get-tuple-element.99) | copy-start | bytes 1815556
  183.7 525.8 %all-gather.5.cloned.1.call-start = ((), (), s32[]{:S(2)}) async-start(), calls=%async_computation.11 | async-start | bytes 1327104 | tf_op jit(solution)/shard_map/all_gather | solution.py:199
  319.3 55.9 %copy-start.26 = (f32[768]{0:T(1024)S(1)}, f32[768]{0:T(1024)}, u32[]{:S(2)}) copy-start(f32[768]{0:T(1024)} %param.28) | copy-start | bytes 9220
  373.1 137.3 %collective-permute-start = (bf16[768,96]{0,1:T(8,128)(2,1)S(1)}, bf16[768,96]{0,1:T(8,128)(2,1)S(1)}, u32[]{:S(2)}, u32[]{:S(2)}) collective-permute-start(bf16[768,96]{0,1:T(8,128)(2,1)S(1)} %get-tuple-element.101), channel_id=1, source_target_pairs={{0,28},{4,0},{8,4},{12,8},{16,12},{20,16},{24,20},{28,24},{1,29},{... | collective-permute-start | bytes 442376 | tf_op jit(solution)/shard_map/ppermute | solution.py:17
  376.4 1.4 copy-start.9
  510.4 135.1 %collective-permute-start.1 = (bf16[768,192]{0,1:T(8,128)(2,1)S(1)}, bf16[768,192]{0,1:T(8,128)(2,1)S(1)}, u32[]{:S(2)}, u32[]{:S(2)}) collective-permute-start(bf16[768,192]{0,1:T(8,128)(2,1)S(1)} %pad_maximum_fusion.1), channel_id=1, source_target_pairs={{0,24},{4,28},{8,0},{12,4},{16,8},{20,12},{24,16},{28,20},{1,25},{... | collective-permute-start | bytes 884744 | tf_op jit(solution)/shard_map/ppermute | solution.py:17
  645.6 59.0 %collective-permute-start.2 = (bf16[768,384]{0,1:T(8,128)(2,1)S(1)}, bf16[768,384]{0,1:T(8,128)(2,1)S(1)}, u32[]{:S(2)}, u32[]{:S(2)}) collective-permute-start(bf16[768,384]{0,1:T(8,128)(2,1)S(1)} %pad_maximum_fusion), channel_id=1, source_target_pairs={{0,16},{4,20},{8,24},{12,28},{16,0},{20,4},{24,8},{28,12},{1,17},{... | collective-permute-start | bytes 1769480 | tf_op jit(solution)/shard_map/ppermute | solution.py:17
  702.2 2.3 copy-start.19
Sparse Core Ops, SparseCore 0:
  22.0 36.4 all-reduce.6
  66.7 34.0 all-reduce.8
  129.7 38.4 all-reduce.10
  171.4 62.2 reduce-scatter.28
  237.3 61.3 reduce-scatter.26
  302.6 68.7 reduce-scatter.20
  374.7 61.3 reduce-scatter.22
  440.1 68.5 reduce-scatter.18
  512.0 62.4 reduce-scatter.24
  578.5 66.0 reduce-scatter.16
  646.8 59.7 all-gather.4
